TPU v7x, 128 devices: a whole 4x4x4 slice. The times are simulated.
128 devices in a mesh: row: 8 (over z, core), col: 16 (over x, y).
Axes of the slice: x: 4, y: 4, z: 4, core: 2. Of those that a mesh axis runs over, the one named last changes fastest.
Arguments:
- tile_values: float32 [2048, 512, 512], P(('row', 'col')), may hold values from -6 to 6
- tile_coords: int32 [2048, 2], P(('row', 'col')), may hold values from 0 to 3, as said below
- tile_counts: int32 [128], P(('row', 'col')), may hold values from 4 to 16, as said below
- restrict_basis: float32 [16384, 256], P(('row', 'col')), may hold values from -0.25 to 0.25
- prolong_basis: float32 [32768, 256], P(('col', 'row')), may hold values from -0.25 to 0.25
- row_partner: int32 [16, 8], replicated, may hold values from 0 to 7, as said below
- col_partner: int32 [8, 16], replicated, may hold values from 0 to 15, as said below
Outputs:
- coarse: float32 [4096, 8192], P('row', 'col')
Inputs may be any that keep to these rules, and one draw needn't show every extreme that they name: `tile_coords`: within one device's 16 slots no two name the same (block row, block column); first entry below 4, second below 4; dead slots also hold such positions. `tile_counts`: number of leading slots of each device that are live; some device has all 16 live. `row_partner`: each row is a pairing: the partner of a part's partner is the part itself, never the part. `col_partner`: each row is a pairing: the partner of a part's partner is the part itself, never the part.
All inputs are finite; a program needn't handle non-finite values.
Results may differ from a plain program's by a relative error of at most 0.0003.
Values sent between devices are 32-bit elements; how exact they have to be, the bound alone decides.
A program may use at most 128 MiB of HBM per device.

v0:
```python
import jax
import jax.numpy as jnp
from jax import lax
from jax.sharding import PartitionSpec as P


def pick_half(block, keep_flag, axis_dim):
    half_size = block.shape[axis_dim] // 2
    first = lax.slice_in_dim(block, 0, half_size, 1, axis_dim)
    second = lax.slice_in_dim(block, half_size, 2 * half_size, 1, axis_dim)
    kept = jnp.where(keep_flag, second, first)
    given = jnp.where(keep_flag, first, second)
    return (kept, given)


def body(
    tile_values, tile_coords, tile_counts, restrict_basis, prolong_basis, row_partner, col_partner
):
    restrict_part = lax.all_gather(restrict_basis, "col", axis=0, tiled=True)
    prolong_part = lax.all_gather(prolong_basis, "row", axis=0, tiled=True)
    tile_order = tile_values.shape[1]
    basis_width = restrict_basis.shape[1]
    block_rows = restrict_part.shape[0] // tile_order
    block_cols = prolong_part.shape[0] // tile_order
    live_count = tile_counts[0]

    def add_slot(slot_index, grid_now):
        block_row = tile_coords[slot_index, 0]
        block_col = tile_coords[slot_index, 1]
        left = lax.dynamic_slice_in_dim(restrict_part, block_row * tile_order, tile_order, 0)
        right = lax.dynamic_slice_in_dim(prolong_part, block_col * tile_order, tile_order, 0)
        applied = jnp.dot(tile_values[slot_index], right, precision=lax.Precision.HIGHEST)
        product = jnp.dot(left.T, applied, precision=lax.Precision.HIGHEST)
        product = jnp.where(slot_index < live_count, product, jnp.zeros_like(product))
        place = (block_row * basis_width, block_col * basis_width)
        current = lax.dynamic_slice(grid_now, place, (basis_width, basis_width))
        return lax.dynamic_update_slice(grid_now, current + product, place)

    start_grid = jnp.zeros((block_rows * basis_width, block_cols * basis_width), jnp.float32)
    local_grid = lax.fori_loop(0, tile_values.shape[0], add_slot, start_grid)
    my_row = lax.axis_index("row")
    my_col = lax.axis_index("col")
    row_table = row_partner[my_col]
    col_table = col_partner[my_row]
    partner_row = row_table[my_row]
    partner_col = col_table[my_col]
    keep_row = my_row > partner_row
    keep_col = my_col > partner_col
    kept, given = pick_half(local_grid, keep_row, 0)
    height = kept.shape[0]
    gathered = lax.all_gather(given, "row", axis=0, tiled=True)
    incoming = lax.dynamic_slice_in_dim(gathered, partner_row * height, height, 0)
    row_section = kept + incoming
    kept, given = pick_half(row_section, keep_col, 1)
    breadth = kept.shape[1]
    gathered = lax.all_gather(given, "col", axis=1, tiled=True)
    incoming = lax.dynamic_slice_in_dim(gathered, partner_col * breadth, breadth, 1)
    return kept + incoming


def solution(mesh):
    in_specs = (
        P(("row", "col"), None, None),
        P(("row", "col"), None),
        P(("row", "col")),
        P(("row", "col"), None),
        P(("col", "row"), None),
        P(),
        P(),
    )
    out_specs = P("row", "col")
    return jax.shard_map(body, mesh=mesh, in_specs=in_specs, out_specs=out_specs, check_vma=False)
```

profile of v0, /device:TPU:1, one launch (start us, length us, event | category | flops | bytes accessed | tf_op | source)
XLA Modules:
  0.0 450.1 jit_solution(11749270185741397715)
XLA Ops:
  6.5 0.7 all-gather.7.cloned.1.call-update
  7.3 0.7 all-gather.5.cloned.1.call-update
  8.1 1.3 dynamic_slice.57
  10.1 28.1 %all-gather.7.cloned.1.call-done = f32[2048,256]{1,0:T(8,128)} async-done(((f32[256,256]{1,0:T(8,128)}), f32[2048,256]{1,0:T(8,128)}) %all-gather.7.cloned.1.call-update) | async-done | bytes 2097168 | tf_op jit(solution)/shard_map/all_gather | solution.py:20
  38.2 45.2 %all-gather.5.cloned.1.call-done = f32[2048,256]{1,0:T(8,128)} async-done(((f32[128,256]{1,0:T(8,128)}), f32[2048,256]{1,0:T(8,128)}) %all-gather.5.cloned.1.call-update) | async-done | bytes 2097168 | tf_op jit(solution)/shard_map/all_gather | solution.py:19
  83.4 2.5 broadcast_in_dim.3
  85.9 148.6 %while.13 = (s32[]{:T(128)}, f32[1024,1024]{1,0:T(8,128)}, s32[16,2]{0,1:T(2,128)S(1)}, s32[]{:T(128)}, f32[2048,256]{1,0:T(8,128)}, /*index=5*/f32[16,512,512]{...) while((s32[]{:T(128)}, f32[1024,1024]{1,0:T(8,128)}, ...), condition=%wide.region_1.2_spmd, body=%wide.region_0.1_spmd.sunk | while | flops 1208090624 | bytes 3670383 | solution.py:40
  86.5 0.7 constant_dynamic-slice_fusion.3
  89.9 2.3 fusion.20
  92.3 2.9 fusion.21
  99.2 2.3 fusion.20
  101.6 2.9 fusion.21
  108.5 2.3 fusion.20
  110.9 2.9 fusion.21
  117.8 2.3 fusion.20
  120.2 2.9 fusion.21
  127.1 2.3 fusion.20
  129.4 2.9 fusion.21
  136.4 2.3 fusion.20
  138.7 2.8 fusion.21
  145.6 2.3 fusion.20
  148.0 2.9 fusion.21
  154.9 2.4 fusion.20
  157.3 2.9 fusion.21
  164.2 2.4 fusion.20
  166.6 2.9 fusion.21
  173.5 2.3 fusion.20
  175.9 2.9 fusion.21
  182.8 2.3 fusion.20
  185.2 2.9 fusion.21
  188.7 0.7 constant_dynamic-slice_fusion.3
  192.1 2.3 fusion.20
  194.5 2.9 fusion.21
  201.4 2.3 fusion.20
  203.7 2.8 fusion.21
  210.6 2.3 fusion.20
  213.0 2.9 fusion.21
  220.0 2.4 fusion.20
  222.3 2.9 fusion.21
  229.2 2.3 fusion.20
  231.6 2.8 fusion.21
  234.4 4.1 slice_select_fusion
  238.6 1.3 dynamic_slice.56
  241.3 83.9 %all-gather.9.cloned.1.call-done = f32[4096,1024]{1,0:T(8,128)} async-done(((f32[512,1024]{1,0:T(8,128)}), f32[4096,1024]{1,0:T(8,128)}) %all-gather.9.cloned.1.call-update) | async-done | bytes 16777232 | tf_op jit(solution)/shard_map/all_gather | solution.py:51
  325.2 3.5 dynamic-slice_add_fusion
  328.8 1.2 slice_select_fusion.1
  330.6 110.5 %all-gather.11.cloned.1.call-done = f32[512,8192]{1,0:T(8,128)} async-done(((f32[512,512]{1,0:T(8,128)}), f32[512,8192]{1,0:T(8,128)}) %all-gather.11.cloned.1.call-update) | async-done | bytes 16777232 | tf_op jit(solution)/shard_map/all_gather | solution.py:56
  441.0 2.5 dynamic-slice_add_fusion.1
  (22 shorter events, 9.5 us)
Async XLA Ops:
  6.5 31.7 %all-gather.7.cloned.1.call-start = ((), (), s32[]{:S(2)}) async-start(), calls=%async_computation.1 | async-start | bytes 2359296 | tf_op jit(solution)/shard_map/all_gather | solution.py:20
  7.3 76.1 %all-gather.5.cloned.1.call-start = ((), (), s32[]{:S(2)}) async-start(), calls=%async_computation | async-start | bytes 2228224 | tf_op jit(solution)/shard_map/all_gather | solution.py:19
  8.0 317.2 %all-gather.9.cloned.1.call-start = ((), (), s32[]{:S(2)}) async-start(), calls=%async_computation.2 | async-start | bytes 18874368 | tf_op jit(solution)/shard_map/all_gather | solution.py:51
  83.4 2.5 copy-start
  238.6 202.4 %all-gather.11.cloned.1.call-start = ((), (), s32[]{:S(2)}) async-start(), calls=%async_computation.3 | async-start | bytes 17825792 | tf_op jit(solution)/shard_map/all_gather | solution.py:56
Sparse Core Ops, SparseCore 0:
  9.0 29.1 all-gather.6
  40.3 43.0 all-gather.4
  238.7 86.4 all-gather.8
  330.1 110.9 all-gather.10
where the time goes:
time: 452 us; the launch traced here: 450 us
  waiting for transfers between devices  269 us (60%)
  matrix products  83.4 us (18%)
  loops' own time  54.4 us (12%)
  local copies, waits for them, and re-layouts  15.9 us (4%)
  between operations  15.8 us (3%)
  other arithmetic  11.4 us (3%)
    all_gather x1, waiting for transfers between devices, body(): gathered = lax.all_gather(given, 'col', axis=1, tiled=True)  110 us
    all_gather x1, waiting for transfers between devices, body(): gathered = lax.all_gather(given, 'row', axis=0, tiled=True)  83.9 us
    another operation x1, loops' own time, body(): local_grid = lax.fori_loop(0, tile_values.shape[0], add_slot, start_grid)  54.4 us
    dot_general x16, matrix products, add_slot(): product = jnp.dot(left.T, applied, precision=lax.Precision.HIGHEST)  45.9 us
    all_gather x1, waiting for transfers between devices, body(): restrict_part = lax.all_gather(restrict_basis, 'col', axis=0, tiled=True)  45.2 us
    dot_general x16, matrix products, add_slot(): jnp.dot(tile_values[slot_index], right, precision=lax.Precision.HIGHEST)  37.6 us
    all_gather x1, waiting for transfers between devices, body(): prolong_part = lax.all_gather(prolong_basis, 'row', axis=0, tiled=True)  28.1 us
    dynamic_slice x16, local copies, waits for them, and re-layouts, add_slot(): block_col = tile_coords[slot_index, 1]  10.7 us
  transfers between devices with their start and end apart: 4, of which 4 were waited for; matrix products, arithmetic and copies ran while one was open for 1% of the time, Pallas kernels for 0%

commit v1 on v0

--- a/solution.py
+++ b/solution.py
@@ -53,7 +53,8 @@
     row_section = kept + incoming
     kept, given = pick_half(row_section, keep_col, 1)
     breadth = kept.shape[1]
-    gathered = lax.all_gather(given, "col", axis=1, tiled=True)
+    sent = jnp.stack([given] * lax.axis_size("col"))
+    gathered = jnp.concatenate(lax.all_to_all(sent, "col", 0, 0), axis=1)
     incoming = lax.dynamic_slice_in_dim(gathered, partner_col * breadth, breadth, 1)
     return kept + incoming
 

time: 452 us -> 729 us (1.61)
  waiting for transfers between devices: 269 us -> 456 us
  local copies, waits for them, and re-layouts: 15.9 us -> 113 us
  matrix products: 83.4 us -> 70.4 us
    all_to_all x0 -> x1, waiting for transfers between devices: none -> 297 us  [body(): gathered = jnp.concatenate(lax.all_to_all(sent, 'col', 0, 0), axis=1)]
    all_gather x1 -> x0, waiting for transfers between devices: 110 us -> none  [body(): gathered = lax.all_gather(given, 'col', axis=1, tiled=True)]
    dynamic_update_slice x0 -> x32, local copies, waits for them, and re-layouts: none -> 52 us  [add_slot(): return lax.dynamic_update_slice(grid_now, current + product, place)]
    dynamic_slice x0 -> x32, local copies, waits for them, and re-layouts: none -> 17.6 us  [add_slot(): current = lax.dynamic_slice(grid_now, place, (basis_width, basis_width))]
    all_to_all x0 -> x1, local copies, waits for them, and re-layouts: none -> 17.6 us  [body(): gathered = jnp.concatenate(lax.all_to_all(sent, 'col', 0, 0), axis=1)]
    dot_general x16, matrix products: 45.9 us -> 32.8 us  [add_slot(): product = jnp.dot(left.T, applied, precision=lax.Precision.HIGHEST)]
    another operation x0 -> x1, local copies, waits for them, and re-layouts: none -> 7.9 us  [body(): sent = jnp.stack([given] * lax.axis_size('col'))]
  transfers between devices with their start and end apart: 4 -> 4, of which waited for: 4 -> 4; matrix products, arithmetic and copies ran while one was open for 1% -> 0% of each run, Pallas kernels for 0% -> 0%
where the time goes in v1:
time: 729 us; the launch traced here: 722 us
  waiting for transfers between devices  456 us (63%)
  local copies, waits for them, and re-layouts  113 us (16%)
  matrix products  70.4 us (10%)
  loops' own time  50.3 us (7%)
  between operations  15.6 us (2%)
  other arithmetic  10.4 us (1%)
    all_to_all x1, waiting for transfers between devices, body(): gathered = jnp.concatenate(lax.all_to_all(sent, 'col', 0, 0), axis=1)  297 us
    all_gather x1, waiting for transfers between devices, body(): gathered = lax.all_gather(given, 'row', axis=0, tiled=True)  84.1 us
    dynamic_update_slice x32, local copies, waits for them, and re-layouts, add_slot(): return lax.dynamic_update_slice(grid_now, current + product, place)  52 us
    another operation x1, loops' own time, body(): local_grid = lax.fori_loop(0, tile_values.shape[0], add_slot, start_grid)  50.3 us
    all_gather x1, waiting for transfers between devices, body(): restrict_part = lax.all_gather(restrict_basis, 'col', axis=0, tiled=True)  45.2 us
    dot_general x16, matrix products, add_slot(): jnp.dot(tile_values[slot_index], right, precision=lax.Precision.HIGHEST)  37.6 us
    dot_general x16, matrix products, add_slot(): product = jnp.dot(left.T, applied, precision=lax.Precision.HIGHEST)  32.8 us
    all_gather x1, waiting for transfers between devices, body(): prolong_part = lax.all_gather(prolong_basis, 'row', axis=0, tiled=True)  28.3 us
  transfers between devices with their start and end apart: 4, of which 4 were waited for; matrix products, arithmetic and copies ran while one was open for 0% of the time, Pallas kernels for 0%

profile of v1, /device:TPU:1, one launch (start us, length us, event | category | flops | bytes accessed | tf_op | source)
XLA Modules:
  0.0 722.5 jit_solution(17819250476489276116)
XLA Ops:
  9.9 28.3 %all-gather.6.cloned.1.call-done = f32[2048,256]{1,0:T(8,128)} async-done(((f32[256,256]{1,0:T(8,128)}), f32[2048,256]{1,0:T(8,128)}) %all-gather.6.cloned.1.call-update) | async-done | bytes 2097168 | tf_op jit(solution)/shard_map/all_gather | solution.py:20
  38.2 45.2 %all-gather.4.cloned.1.call-done = f32[2048,256]{1,0:T(8,128)} async-done(((f32[128,256]{1,0:T(8,128)}), f32[2048,256]{1,0:T(8,128)}) %all-gather.4.cloned.1.call-update) | async-done | bytes 2097168 | tf_op jit(solution)/shard_map/all_gather | solution.py:19
  83.4 2.5 broadcast_in_dim.3.clone
  85.9 200.8 %while.13 = (s32[]{:T(128)}, f32[1024,1024]{0,1:T(8,128)}, s32[16,2]{0,1:T(2,128)S(1)}, s32[]{:T(128)}, f32[2048,256]{1,0:T(8,128)}, /*index=5*/f32[16,512,512]{...) while((s32[]{:T(128)}, f32[1024,1024]{0,1:T(8,128)}, ...), condition=%wide.region_1.2_spmd, body=%wide.region_0.1_spmd.sunk | while | flops 1208090624 | bytes 5767535 | solution.py:40
  90.7 2.4 fusion.19
  95.3 2.9 dynamic_update_slice.8
  103.1 2.3 fusion.19
  105.4 2.1 fusion.20
  107.6 2.4 dynamic_update_slice.8
  114.9 2.4 fusion.19
  119.5 3.6 dynamic_update_slice.8
  127.9 2.3 fusion.19
  132.5 2.9 dynamic_update_slice.8
  140.2 2.3 fusion.19
  142.6 2.1 fusion.20
  144.8 3.6 dynamic_update_slice.8
  153.2 2.3 fusion.19
  157.8 3.6 dynamic_update_slice.8
  166.3 2.3 fusion.19
  168.6 2.1 fusion.20
  170.8 3.6 dynamic_update_slice.8
  179.3 2.3 fusion.19
  181.6 2.1 fusion.20
  183.8 3.6 dynamic_update_slice.8
  192.2 2.4 fusion.19
  196.8 2.4 dynamic_update_slice.8
  204.0 2.3 fusion.19
  206.4 2.1 fusion.20
  208.6 3.5 dynamic_update_slice.8
  217.0 2.3 fusion.19
  219.3 2.1 fusion.20
  221.5 3.6 dynamic_update_slice.8
  230.0 2.3 fusion.19
  234.6 3.6 dynamic_update_slice.8
  243.0 2.3 fusion.19
  254.4 2.3 fusion.19
  259.0 3.6 dynamic_update_slice.8
  267.4 2.3 fusion.19
  272.0 2.9 dynamic_update_slice.8
  279.7 2.3 fusion.19
  284.3 2.4 dynamic_update_slice.8
  286.7 4.0 slice_select_fusion
  293.2 84.1 %all-gather.8.cloned.1.call-done = f32[4096,1024]{0,1:T(8,128)} async-done(((f32[512,1024]{0,1:T(8,128)}), f32[4096,1024]{0,1:T(8,128)}) %all-gather.8.cloned.1.call-update) | async-done | bytes 16777232 | tf_op jit(solution)/shard_map/all_gather | solution.py:51
  377.4 3.6 dynamic-slice_add_fusion
  383.7 7.9 %stack.2 = f32[16,512,512]{2,1,0:T(8,128)} broadcast(f32[512,512]{1,0:T(8,128)S(1)} %copy.10), dimensions={1,2} | broadcast | bytes 17825792 | tf_op jit(solution)/shard_map/stack | solution.py:56
  391.6 6.6 all-to-all-start
  398.8 296.6 %all-to-all-done = f32[16,512,512]{2,1,0:T(8,128)} async-done(((f32[16,512,512]{2,1,0:T(8,128)}), f32[16,512,512]{2,1,0:T(8,128)}, u32[]{:S(2)}, u32[]{:S(2)}) %all-to-all-start) | async-done | bytes 16777248 | tf_op jit(solution)/shard_map/all_to_all | solution.py:57
  695.5 17.6 %copy.11 = f32[16,512,512]{1,2,0:T(8,128)} copy(f32[16,512,512]{2,1,0:T(8,128)} %all-to-all-done) | data formatting | bytes 33554432 | tf_op jit(solution)/shard_map/all_to_all | solution.py:57
  (89 shorter events, 62.3 us)
Async XLA Ops:
  6.5 31.7 %all-gather.6.cloned.1.call-start = ((), (), s32[]{:S(2)}) async-start(), calls=%async_computation.2 | async-start | bytes 2359296 | tf_op jit(solution)/shard_map/all_gather | solution.py:20
  7.3 76.1 %all-gather.4.cloned.1.call-start = ((), (), s32[]{:S(2)}) async-start(), calls=%async_computation.1 | async-start | bytes 2228224 | tf_op jit(solution)/shard_map/all_gather | solution.py:19
  8.0 369.4 %all-gather.8.cloned.1.call-start = ((), (), s32[]{:S(2)}) async-start(), calls=%async_computation.3 | async-start | bytes 18874368 | tf_op jit(solution)/shard_map/all_gather | solution.py:51
  83.4 2.5 copy-start
  391.6 303.8 %all-to-all-start = ((f32[16,512,512]{2,1,0:T(8,128)}), f32[16,512,512]{2,1,0:T(8,128)}, u32[]{:S(2)}, u32[]{:S(2)}) async-start(f32[16,512,512]{2,1,0:T(8,128)} %stack.2), calls=%async_computation | async-start | bytes 33554432 | tf_op jit(solution)/shard_map/all_to_all | solution.py:57
Sparse Core Ops, SparseCore 0:
  9.0 29.1 all-gather.5
  40.3 43.0 all-gather.3
  290.9 86.4 all-gather.7
